TPU v7x, 256 devices: a whole 4x4x8 slice. The times are simulated.
256 devices in a mesh: region: 32 (over x, z), comm: 8 (over y, core).
Axes of the slice: x: 4, y: 4, z: 8, core: 2. Of those that a mesh axis runs over, the one named last changes fastest.
Arguments:
- cost: float32 [128, 262144], P('comm', 'region'), may hold values from 0.01 to 15, as said below
- flow_start: float32 [128, 262144], P('comm', 'region'), may hold values from 0 to 0.5
- capacity: float32 [262144], P('region'), may hold values from 5 to 135, as said below
- cap_dual_start: float32 [262144], P('region'), may hold values from 0 to 1
- demand: float32 [128, 131072], P('comm', 'region'), may hold values from -24 to 24
- node_dual_start: float32 [128, 131072], P('comm', 'region'), may hold values from -6 to 6
- incidence: float32 [4096, 128, 128], P('region'), may hold values from -0.25 to 0.25
- block_node: int32 [4096], P('region'), may hold values from 0 to 39
- ghost_source: int32 [256], P('region'), may hold values from 0 to 127, as said below
Outputs:
- final_flow: float32 [128, 262144], P('comm', 'region')
- final_cap_dual: float32 [262144], P('region')
- final_node_dual: float32 [128, 131072], P('comm', 'region')
Inputs may be any that keep to these rules, and one draw needn't show every extreme that they name: Each cost is positive. Each capacity is positive. `ghost_source`: ghost slot g of region r names boundary block j of region q as q * 4 + j. Slot 0 of every region has q = r + 16 in cyclic order; every other slot has q at most two regions from r in cyclic order (q may be r).
All inputs are finite; a program needn't handle non-finite values.
Results may differ from a plain program's by a relative error of at most 0.00021.
Values sent between devices are 32-bit elements; how exact they have to be, the bound alone decides.
A program may use at most 64 MiB of HBM per device.

v0:
```python
import jax
import jax.numpy as jnp
from jax import lax
from jax.sharding import PartitionSpec as P

BPA = 2
NBD = 4
NG = 8
ITERS = 2
step_scale = 0.08
highest = lax.Precision.HIGHEST


def pick_blocks(bnd_table, indices, commodities, count, block_width):
    return jnp.take(bnd_table.reshape(commodities, count, block_width), indices, axis=1)


def body(
    cost,
    flow_start,
    capacity,
    cap_dual_start,
    demand,
    node_dual_start,
    incidence,
    block_node,
    ghost_source,
):
    commodities, arc_count = cost.shape
    block_count, block_width, _ = incidence.shape
    own_blocks = demand.shape[1] // block_width
    region_total = lax.axis_size("region")
    bound_all = region_total * NBD
    slot_count = own_blocks + NG
    cost_sq = jnp.sum(cost * cost)
    demand_sq = jnp.sum(demand * demand)
    capacity_sq = jnp.sum(capacity * capacity)
    cost_all, demand_all = lax.psum((cost_sq, demand_sq), ("region", "comm"))
    capacity_all = lax.psum(capacity_sq, "region")
    weight = jnp.sqrt(cost_all / (demand_all + capacity_all))
    primal_step = step_scale / weight
    dual_step = step_scale * weight
    slot_table = (block_node[:, None] == jnp.arange(slot_count, dtype=jnp.int32)[None, :]).astype(
        jnp.float32
    )
    ghost_table = (ghost_source[:, None] == jnp.arange(bound_all, dtype=jnp.int32)[None, :]).astype(
        jnp.float32
    )
    flow_now, cap_dual, node_dual = (flow_start, cap_dual_start, node_dual_start)
    edge_cols = NBD * block_width
    for iteration in range(ITERS):
        bnd_table = lax.all_gather(node_dual[:, :edge_cols], "region", axis=1, tiled=True)
        ghost_duals = pick_blocks(bnd_table, ghost_source, commodities, bound_all, block_width)
        dual_blocks = jnp.concatenate(
            [node_dual.reshape(commodities, own_blocks, block_width), ghost_duals], axis=1
        )
        chosen_duals = jnp.take(dual_blocks, block_node, axis=1)
        back_term = jnp.einsum("kbn,bna->kba", chosen_duals, incidence, precision=highest)
        back_term = (
            back_term.reshape(commodities, block_count // BPA, BPA, block_width)
            .sum(axis=2)
            .reshape(commodities, arc_count)
        )
        flow_new = jnp.maximum(flow_now - primal_step * (cost - back_term + cap_dual[None, :]), 0.0)
        flow_bar = 2.0 * flow_new - flow_now
        arc_load = jnp.sum(flow_bar, axis=0)
        load_total = lax.psum(arc_load, "comm")
        cap_dual = jnp.maximum(cap_dual + dual_step * (load_total - capacity), 0.0)
        repeated_flow = jnp.repeat(
            flow_bar.reshape(commodities, arc_count // block_width, block_width), BPA, axis=1
        )
        forward = jnp.einsum("kba,bna->kbn", repeated_flow, incidence, precision=highest)
        slot_rows = jnp.einsum("kbn,bs->ksn", forward, slot_table, precision=highest)
        own_rows = slot_rows[:, :own_blocks]
        routed = jnp.einsum(
            "kgn,gb->kbn", slot_rows[:, own_blocks:], ghost_table, precision=highest
        )
        arrived = lax.psum_scatter(routed, "region", scatter_dimension=1, tiled=True)
        node_rows = jnp.concatenate([own_rows[:, :NBD] + arrived, own_rows[:, NBD:]], axis=1)
        node_dual = node_dual + dual_step * (
            demand - node_rows.reshape(commodities, own_blocks * block_width)
        )
        flow_now = flow_new
    return (flow_now, cap_dual, node_dual)


def solution(mesh):
    return jax.shard_map(
        body,
        mesh=mesh,
        in_specs=(
            P("comm", "region"),
            P("comm", "region"),
            P("region"),
            P("region"),
            P("comm", "region"),
            P("comm", "region"),
            P("region", None, None),
            P("region"),
            P("region"),
        ),
        out_specs=(P("comm", "region"), P("region"), P("comm", "region")),
        check_vma=False,
    )
```

profile of v0, /device:TPU:8, one launch (start us, length us, event | category | flops | bytes accessed | tf_op | source)
XLA Modules:
  0.0 738.6 jit_solution(913210635620972559)
XLA Ops:
  7.2 1.5 slice.30
  8.8 1.6 multiply_reduce_fusion.1
  10.4 1.8 multiply_reduce_fusion
  12.2 1.4 multiply_reduce_fusion.2
  13.6 79.2 %all-reduce = (f32[]{:T(128)}, f32[]{:T(128)}) all-reduce(f32[]{:T(128)} %multiply_reduce_fusion, f32[]{:T(128)} %multiply_reduce_fusion.1), channel_id=1, replica_groups=mesh['region'=32,'comm'=8] {'region','comm'}, use_global_device_ids=true, to_apply=%region_1.0 | all-reduce | flops 2 | bytes 16 | tf_op jit(solution)/shard_map/psum | solution.py:38
  92.9 73.2 %psum.37 = f32[]{:T(128)} all-reduce(f32[]{:T(128)} %multiply_reduce_fusion.2), channel_id=1, replica_groups=mesh['region'=32,'comm'=8] {'region'}, use_global_device_ids=true, to_apply=%region_5.0 | all-reduce | flops 1 | bytes 8 | tf_op jit(solution)/shard_map/psum | solution.py:39
  168.2 0.7 compare_select_fusion.1
  169.5 0.7 compare_and_fusion
  170.1 0.7 compare_and_fusion.1
  170.8 1.0 copy_bitcast_fusion.5
  171.8 1.3 copy_bitcast_fusion.1
  173.8 0.8 gather_fusion.1
  174.6 9.6 %bitcast_reduce_fusion.1 = f32[16,64,128]{2,0,1:T(8,128)S(1)} fusion(f32[128,128,128]{2,1,0:T(8,128)} %param.19, f32[128,16,128]{2,1,0:T(8,128)S(1)} %gather_fusion.1, pred[128]{0:T(512)(128)(4,1)S(1)} %compare_and_fusion), kind=kOutput, calls=%fused_computation.13 | convolution fusion | flops 403046400 | bytes 9961600 | tf_op jit(solution)/shard_map/kbn,bna->kba/dot_general | solution.py:58
  184.7 15.4 %convolution_bitcast_fusion.1 = f32[16,128,128]{2,0,1:T(8,128)S(1)} fusion(f32[16,128,128]{2,0,1:T(8,128)S(1)} %bitcast.122, f32[128,128,128]{2,1,0:T(8,128)} %param.19), kind=kOutput, calls=%fused_computation.5 | convolution fusion | flops 402653184 | bytes 10485760 | tf_op jit(solution)/shard_map/kba,bna->kbn/dot_general | solution.py:72
  200.1 0.8 convolution_bitcast_fusion.5
  200.9 0.7 convolution_bitcast_fusion.3
  201.6 1.6 copy.37
  203.3 206.3 %reduce-scatter.3.cloned.1.call-done = f32[16,4,128]{2,0,1:T(8,128)} async-done(((f32[16,128,128]{2,0,1:T(8,128)}), f32[16,4,128]{2,0,1:T(8,128)}) %reduce-scatter.3.cloned.1.call-update) | async-done | bytes 32784 | tf_op jit(solution)/shard_map/reduce_scatter | solution.py:78
  409.6 0.8 slice_add_fusion.1
  411.3 20.9 %psum.38 = f32[8192]{0:T(1024)S(1)} all-reduce(f32[8192]{0:T(1024)S(1)} %get-tuple-element.9), channel_id=1, replica_groups=mesh['region'=32,'comm'=8] {'comm'}, use_global_device_ids=true, to_apply=%region_10.13 | all-reduce | flops 8192 | bytes 65536 | tf_op jit(solution)/shard_map/psum | solution.py:67
  432.2 55.1 %all-gather.5.cloned.1.call-done = f32[16,16384]{1,0:T(8,128)} async-done(((f32[16,512]{1,0:T(8,128)}), f32[16,16384]{1,0:T(8,128)}) %all-gather.5.cloned.1.call-update) | async-done | bytes 1048592 | tf_op jit(solution)/shard_map/all_gather | solution.py:52
  487.3 1.3 copy_bitcast_fusion
  489.3 0.8 gather_fusion.3
  490.1 9.6 %bitcast_reduce_fusion = f32[16,64,128]{2,0,1:T(8,128)S(1)} fusion(f32[128,128,128]{2,1,0:T(8,128)} %param.19, f32[128,16,128]{2,1,0:T(8,128)S(1)} %gather_fusion.3, pred[128]{0:T(512)(128)(4,1)S(1)} %compare_and_fusion), kind=kOutput, calls=%fused_computation.12 | convolution fusion | flops 403046400 | bytes 9961600 | tf_op jit(solution)/shard_map/kbn,bna->kba/dot_general | solution.py:58
  500.0 15.4 %convolution_bitcast_fusion = f32[16,128,128]{2,0,1:T(8,128)S(1)} fusion(f32[16,128,128]{2,0,1:T(8,128)S(1)} %bitcast.123, f32[128,128,128]{2,1,0:T(8,128)} %param.19), kind=kOutput, calls=%fused_computation.4 | convolution fusion | flops 402653184 | bytes 10485760 | tf_op jit(solution)/shard_map/kba,bna->kbn/dot_general | solution.py:72
  515.4 0.8 convolution_bitcast_fusion.4
  516.2 0.7 convolution_bitcast_fusion.2
  516.9 1.6 copy.44
  518.7 20.7 %psum.39 = f32[8192]{0:T(1024)S(1)} all-reduce(f32[8192]{0:T(1024)S(1)} %fusion.31), channel_id=1, replica_groups=mesh['region'=32,'comm'=8] {'comm'}, use_global_device_ids=true, to_apply=%region_12.15 | all-reduce | flops 8192 | bytes 65536 | tf_op jit(solution)/shard_map/psum | solution.py:67
  540.0 190.4 %reduce-scatter.5.cloned.1.call-done = f32[16,4,128]{2,0,1:T(8,128)} async-done(((f32[16,128,128]{2,0,1:T(8,128)}), f32[16,4,128]{2,0,1:T(8,128)}) %reduce-scatter.5.cloned.1.call-update) | async-done | bytes 32784 | tf_op jit(solution)/shard_map/reduce_scatter | solution.py:78
  730.3 0.8 slice_add_fusion
  731.1 0.9 fusion.25
  (52 shorter events, 4.6 us)
Async XLA Ops:
  7.2 177.0 %copy-start = (f32[16,8192]{1,0:T(8,128)S(1)}, f32[16,8192]{1,0:T(8,128)}, u32[]{:S(2)}) copy-start(f32[16,8192]{1,0:T(8,128)} %param.13) | copy-start | bytes 1572868
  7.2 177.0 %copy-start.6 = (f32[8192]{0:T(1024)S(1)}, f32[8192]{0:T(1024)}, u32[]{:S(2)}) copy-start(f32[8192]{0:T(1024)} %param.16) | copy-start | bytes 98308
  7.2 177.0 %copy-start.2 = (f32[16,8192]{1,0:T(8,128)S(1)}, f32[16,8192]{1,0:T(8,128)}, u32[]{:S(2)}) copy-start(f32[16,8192]{1,0:T(8,128)} %param.14) | copy-start | bytes 1572868
  7.2 164.6 %all-gather.3.cloned.1.call-start = ((), (), s32[]{:S(2)}) async-start(), calls=%async_computation.2 | async-start | bytes 1081344 | tf_op jit(solution)/shard_map/all_gather | solution.py:52
  8.7 400.9 %reduce-scatter.3.cloned.1.call-start = ((), (), s32[]{:S(2)}) async-start(), calls=%async_computation.3 | async-start | bytes 1081344 | tf_op jit(solution)/shard_map/reduce_scatter | solution.py:78
  184.2 15.9 %copy-start.7 = (s32[128]{0:T(128)S(1)}, s32[128]{0:T(128)}, u32[]{:S(2)}) copy-start(s32[128]{0:T(128)} %param.20) | copy-start | bytes 1540
  184.2 16.6 %copy-start.8 = (s32[8]{0:T(128)S(1)}, s32[8]{0:T(128)}, u32[]{:S(2)}) copy-start(s32[8]{0:T(128)} %param.21) | copy-start | bytes 100
  184.6 225.8 %copy-start.1 = (f32[16,4096]{1,0:T(8,128)S(1)}, f32[16,4096]{1,0:T(8,128)}, u32[]{:S(2)}) copy-start(f32[16,4096]{1,0:T(8,128)} %param.17) | copy-start | bytes 786436
  184.6 225.8 %copy-start.4 = (f32[16,4096]{1,0:T(8,128)S(1)}, f32[16,4096]{1,0:T(8,128)}, u32[]{:S(2)}) copy-start(f32[16,4096]{1,0:T(8,128)} %param.18) | copy-start | bytes 786436
  184.6 247.5 %copy-start.5 = (f32[8192]{0:T(1024)S(1)}, f32[8192]{0:T(1024)}, u32[]{:S(2)}) copy-start(f32[8192]{0:T(1024)} %param.15) | copy-start | bytes 98308
  203.2 284.1 %all-gather.5.cloned.1.call-start = ((), (), s32[]{:S(2)}) async-start(), calls=%async_computation.4 | async-start | bytes 1081344 | tf_op jit(solution)/shard_map/all_gather | solution.py:52
  411.3 319.1 %reduce-scatter.5.cloned.1.call-start = ((), (), s32[]{:S(2)}) async-start(), calls=%async_computation.5 | async-start | bytes 1081344 | tf_op jit(solution)/shard_map/reduce_scatter | solution.py:78
  499.8 18.7 %copy-start.3 = (f32[16,8192]{1,0:T(8,128)}, f32[16,8192]{1,0:T(8,128)S(1)}, u32[]{:S(2)}) copy-start(f32[16,8192]{1,0:T(8,128)S(1)} %get-tuple-element.8) | copy-start | bytes 1572868
Sparse Core Ops, SparseCore 0:
  11.2 78.9 all-gather.2
  203.3 206.2 reduce-scatter.2
  412.8 74.4 all-gather.4
  518.6 211.6 reduce-scatter.4
where the time goes:
time: 739 us
  waiting for transfers between devices  452 us (61%)
  blocking collectives  194 us (26%)
  matrix products  53 us (7%)
  between operations  16.2 us (2%)
  local copies, waits for them, and re-layouts  11.8 us (2%)
  other arithmetic  11.5 us (2%)
    reduce_scatter x2, waiting for transfers between devices, body(): lax.psum_scatter(routed, 'region', scatter_dimension=1, tiled=True)  397 us
    psum x1, blocking collectives, body(): cost_all, demand_all = lax.psum((cost_sq, demand_sq), ('region', 'comm'))  79.2 us
    psum x1, blocking collectives, body(): capacity_all = lax.psum(capacity_sq, 'region')  73.2 us
    all_gather x2, waiting for transfers between devices, body(): lax.all_gather(node_dual[:, :edge_cols], 'region', axis=1, tiled=True)  55.1 us
    psum x2, blocking collectives, body(): load_total = lax.psum(arc_load, 'comm')  41.5 us
    dot_general x2, matrix products, body(): jnp.einsum('kba,bna->kbn', repeated_flow, incidence, precision=highest)  30.9 us
    dot_general x2, matrix products, body(): jnp.einsum('kbn,bna->kba', chosen_duals, incidence, precision=highest)  19.2 us
  transfers between devices with their start and end apart: 4, of which 3 were waited for; matrix products, arithmetic and copies ran while one was open for 1% of the time, Pallas kernels for 0%

commit v1 on v0

--- a/solution.py
+++ b/solution.py
@@ -35,7 +35,7 @@
     cost_sq = jnp.sum(cost * cost)
     demand_sq = jnp.sum(demand * demand)
     capacity_sq = jnp.sum(capacity * capacity)
-    cost_all, demand_all = lax.psum((cost_sq, demand_sq), ("region", "comm"))
+    cost_all, demand_all = lax.psum(lax.psum((cost_sq, demand_sq), "region"), "comm")
     capacity_all = lax.psum(capacity_sq, "region")
     weight = jnp.sqrt(cost_all / (demand_all + capacity_all))
     primal_step = step_scale / weight

time: 739 us -> 677 us (0.916)
  blocking collectives: 194 us -> 130 us
    psum x2, blocking collectives: 152 us -> 89 us  [the longest x1 78.4 us: body(): lax.psum((cost_sq, demand_sq), 'region')]
where the time goes in v1:
time: 677 us
  waiting for transfers between devices  453 us (67%)
  blocking collectives  130 us (19%)
  matrix products  53 us (8%)
  between operations  16.2 us (2%)
  local copies, waits for them, and re-layouts  11.8 us (2%)
  other arithmetic  11.5 us (2%)
    reduce_scatter x2, waiting for transfers between devices, body(): lax.psum_scatter(routed, 'region', scatter_dimension=1, tiled=True)  398 us
    psum x1, blocking collectives, body(): lax.psum((cost_sq, demand_sq), 'region')  78.4 us
    all_gather x2, waiting for transfers between devices, body(): lax.all_gather(node_dual[:, :edge_cols], 'region', axis=1, tiled=True)  55.1 us
    psum x2, blocking collectives, body(): load_total = lax.psum(arc_load, 'comm')  41.5 us
    dot_general x2, matrix products, body(): jnp.einsum('kba,bna->kbn', repeated_flow, incidence, precision=highest)  30.9 us
    dot_general x2, matrix products, body(): jnp.einsum('kbn,bna->kba', chosen_duals, incidence, precision=highest)  19.2 us
  transfers between devices with their start and end apart: 4, of which 3 were waited for; matrix products, arithmetic and copies ran while one was open for 1% of the time, Pallas kernels for 0%

profile of v1, /device:TPU:8, one launch (start us, length us, event | category | flops | bytes accessed | tf_op | source)
XLA Modules:
  0.0 676.6 jit_solution(1180435913589919938)
XLA Ops:
  7.2 1.5 slice.30
  8.8 1.6 multiply_reduce_fusion.1
  10.4 1.8 multiply_reduce_fusion
  12.2 1.4 multiply_reduce_fusion.2
  13.6 78.4 %all-reduce = (f32[]{:T(128)}, f32[]{:T(128)}, f32[]{:T(128)}) all-reduce(f32[]{:T(128)} %multiply_reduce_fusion, f32[]{:T(128)} %multiply_reduce_fusion.1, f32[]{:T(128)} %multiply_reduce_fusion.2), channel_id=1, replica_groups=mesh['region'=32,'comm'=8] {'region'}, use_global_device_ids=true, to_apply=%region_1.0 | all-reduce | flops 3 | bytes 24 | tf_op jit(solution)/shard_map/psum | solution.py:38
  92.0 10.6 %all-reduce.1 = (f32[]{:T(128)}, f32[]{:T(128)}) all-reduce(f32[]{:T(128)} %get-tuple-element.5, f32[]{:T(128)} %get-tuple-element.6), channel_id=1, replica_groups=mesh['region'=32,'comm'=8] {'comm'}, use_global_device_ids=true, to_apply=%region_2.0 | all-reduce | flops 2 | bytes 16 | tf_op jit(solution)/shard_map/psum | solution.py:38
  104.7 0.7 compare_select_fusion.1
  106.0 0.7 compare_and_fusion
  106.7 0.7 compare_and_fusion.1
  107.4 1.0 copy_bitcast_fusion.5
  108.4 1.3 copy_bitcast_fusion.1
  110.3 0.8 gather_fusion.1
  111.1 9.6 %bitcast_reduce_fusion.1 = f32[16,64,128]{2,0,1:T(8,128)S(1)} fusion(f32[128,128,128]{2,1,0:T(8,128)} %param.19, f32[128,16,128]{2,1,0:T(8,128)S(1)} %gather_fusion.1, pred[128]{0:T(512)(128)(4,1)S(1)} %compare_and_fusion), kind=kOutput, calls=%fused_computation.13 | convolution fusion | flops 403046400 | bytes 9961600 | tf_op jit(solution)/shard_map/kbn,bna->kba/dot_general | solution.py:58
  121.2 15.4 %convolution_bitcast_fusion.1 = f32[16,128,128]{2,0,1:T(8,128)S(1)} fusion(f32[16,128,128]{2,0,1:T(8,128)S(1)} %bitcast.122, f32[128,128,128]{2,1,0:T(8,128)} %param.19), kind=kOutput, calls=%fused_computation.5 | convolution fusion | flops 402653184 | bytes 10485760 | tf_op jit(solution)/shard_map/kba,bna->kbn/dot_general | solution.py:72
  136.6 0.8 convolution_bitcast_fusion.5
  137.4 0.7 convolution_bitcast_fusion.3
  138.1 1.6 copy.37
  139.8 208.0 %reduce-scatter.3.cloned.1.call-done = f32[16,4,128]{2,0,1:T(8,128)} async-done(((f32[16,128,128]{2,0,1:T(8,128)}), f32[16,4,128]{2,0,1:T(8,128)}) %reduce-scatter.3.cloned.1.call-update) | async-done | bytes 32784 | tf_op jit(solution)/shard_map/reduce_scatter | solution.py:78
  347.8 0.8 slice_add_fusion.1
  349.5 20.8 %psum.54 = f32[8192]{0:T(1024)S(1)} all-reduce(f32[8192]{0:T(1024)S(1)} %get-tuple-element.12), channel_id=1, replica_groups=mesh['region'=32,'comm'=8] {'comm'}, use_global_device_ids=true, to_apply=%region_12.15 | all-reduce | flops 8192 | bytes 65536 | tf_op jit(solution)/shard_map/psum | solution.py:67
  370.3 55.0 %all-gather.5.cloned.1.call-done = f32[16,16384]{1,0:T(8,128)} async-done(((f32[16,512]{1,0:T(8,128)}), f32[16,16384]{1,0:T(8,128)}) %all-gather.5.cloned.1.call-update) | async-done | bytes 1048592 | tf_op jit(solution)/shard_map/all_gather | solution.py:52
  425.4 1.3 copy_bitcast_fusion
  427.3 0.8 gather_fusion.3
  428.1 9.6 %bitcast_reduce_fusion = f32[16,64,128]{2,0,1:T(8,128)S(1)} fusion(f32[128,128,128]{2,1,0:T(8,128)} %param.19, f32[128,16,128]{2,1,0:T(8,128)S(1)} %gather_fusion.3, pred[128]{0:T(512)(128)(4,1)S(1)} %compare_and_fusion), kind=kOutput, calls=%fused_computation.12 | convolution fusion | flops 403046400 | bytes 9961600 | tf_op jit(solution)/shard_map/kbn,bna->kba/dot_general | solution.py:58
  438.0 15.4 %convolution_bitcast_fusion = f32[16,128,128]{2,0,1:T(8,128)S(1)} fusion(f32[16,128,128]{2,0,1:T(8,128)S(1)} %bitcast.123, f32[128,128,128]{2,1,0:T(8,128)} %param.19), kind=kOutput, calls=%fused_computation.4 | convolution fusion | flops 402653184 | bytes 10485760 | tf_op jit(solution)/shard_map/kba,bna->kbn/dot_general | solution.py:72
  453.5 0.8 convolution_bitcast_fusion.4
  454.2 0.7 convolution_bitcast_fusion.2
  454.9 1.6 copy.44
  456.7 20.7 %psum.55 = f32[8192]{0:T(1024)S(1)} all-reduce(f32[8192]{0:T(1024)S(1)} %fusion.31), channel_id=1, replica_groups=mesh['region'=32,'comm'=8] {'comm'}, use_global_device_ids=true, to_apply=%region_14.17 | all-reduce | flops 8192 | bytes 65536 | tf_op jit(solution)/shard_map/psum | solution.py:67
  478.0 190.3 %reduce-scatter.5.cloned.1.call-done = f32[16,4,128]{2,0,1:T(8,128)} async-done(((f32[16,128,128]{2,0,1:T(8,128)}), f32[16,4,128]{2,0,1:T(8,128)}) %reduce-scatter.5.cloned.1.call-update) | async-done | bytes 32784 | tf_op jit(solution)/shard_map/reduce_scatter | solution.py:78
  668.3 0.8 slice_add_fusion
  669.2 0.9 fusion.25
  (52 shorter events, 4.6 us)
Async XLA Ops:
  7.2 113.6 %copy-start = (f32[16,8192]{1,0:T(8,128)S(1)}, f32[16,8192]{1,0:T(8,128)}, u32[]{:S(2)}) copy-start(f32[16,8192]{1,0:T(8,128)} %param.13) | copy-start | bytes 1572868
  7.2 113.6 %copy-start.6 = (f32[8192]{0:T(1024)S(1)}, f32[8192]{0:T(1024)}, u32[]{:S(2)}) copy-start(f32[8192]{0:T(1024)} %param.16) | copy-start | bytes 98308
  7.2 113.6 %copy-start.2 = (f32[16,8192]{1,0:T(8,128)S(1)}, f32[16,8192]{1,0:T(8,128)}, u32[]{:S(2)}) copy-start(f32[16,8192]{1,0:T(8,128)} %param.14) | copy-start | bytes 1572868
  7.2 101.2 %all-gather.3.cloned.1.call-start = ((), (), s32[]{:S(2)}) async-start(), calls=%async_computation.2 | async-start | bytes 1081344 | tf_op jit(solution)/shard_map/all_gather | solution.py:52
  8.7 339.1 %reduce-scatter.3.cloned.1.call-start = ((), (), s32[]{:S(2)}) async-start(), calls=%async_computation.3 | async-start | bytes 1081344 | tf_op jit(solution)/shard_map/reduce_scatter | solution.py:78
  120.8 15.9 %copy-start.7 = (s32[128]{0:T(128)S(1)}, s32[128]{0:T(128)}, u32[]{:S(2)}) copy-start(s32[128]{0:T(128)} %param.20) | copy-start | bytes 1540
  120.8 16.6 %copy-start.8 = (s32[8]{0:T(128)S(1)}, s32[8]{0:T(128)}, u32[]{:S(2)}) copy-start(s32[8]{0:T(128)} %param.21) | copy-start | bytes 100
  121.2 227.4 %copy-start.1 = (f32[16,4096]{1,0:T(8,128)S(1)}, f32[16,4096]{1,0:T(8,128)}, u32[]{:S(2)}) copy-start(f32[16,4096]{1,0:T(8,128)} %param.17) | copy-start | bytes 786436
  121.2 227.4 %copy-start.4 = (f32[16,4096]{1,0:T(8,128)S(1)}, f32[16,4096]{1,0:T(8,128)}, u32[]{:S(2)}) copy-start(f32[16,4096]{1,0:T(8,128)} %param.18) | copy-start | bytes 786436
  121.2 249.1 %copy-start.5 = (f32[8192]{0:T(1024)S(1)}, f32[8192]{0:T(1024)}, u32[]{:S(2)}) copy-start(f32[8192]{0:T(1024)} %param.15) | copy-start | bytes 98308
  139.7 285.6 %all-gather.5.cloned.1.call-start = ((), (), s32[]{:S(2)}) async-start(), calls=%async_computation.4 | async-start | bytes 1081344 | tf_op jit(solution)/shard_map/all_gather | solution.py:52
  349.4 318.9 %reduce-scatter.5.cloned.1.call-start = ((), (), s32[]{:S(2)}) async-start(), calls=%async_computation.5 | async-start | bytes 1081344 | tf_op jit(solution)/shard_map/reduce_scatter | solution.py:78
  437.9 18.7 %copy-start.3 = (f32[16,8192]{1,0:T(8,128)}, f32[16,8192]{1,0:T(8,128)S(1)}, u32[]{:S(2)}) copy-start(f32[16,8192]{1,0:T(8,128)S(1)} %get-tuple-element.11) | copy-start | bytes 1572868
Sparse Core Ops, SparseCore 0:
  11.2 78.9 all-gather.2
  139.9 207.8 reduce-scatter.2
  351.0 74.3 all-gather.4
  456.7 211.6 reduce-scatter.4
